TPU v7x, 256 devices: a whole 4x4x8 slice. The times are simulated.
256 devices in a mesh: hel: 16 (over z_lo, x, core), rad: 16 (over z_hi, y).
Axes of the slice: x: 4, y: 4, z: 8 (z_hi: 4, z_lo: 2; z = z_hi * 2 + z_lo), core: 2. Of those that a mesh axis runs over, the one named last changes fastest.
Arguments:
- packet: bfloat16 [1024, 2, 64, 4, 512], P('rad', None, 'hel'), may hold values from -6 to 6
- first_propagator: bfloat16 [2, 1024, 1024], replicated, may hold values from -0.125 to 0.125
- second_propagator: bfloat16 [2, 512, 512], replicated, may hold values from -0.1875 to 0.1875
- potential: float32 [1024, 4, 512], P('rad'), may hold values from -3.140625 to 3.140625
- coupling: float32 [64, 4], replicated, may hold values from 0.2 to 0.8
- radial_weight: float32 [1024, 512], P('rad'), may hold values from 0.25 to 1
Outputs:
- advanced: bfloat16 [1024, 2, 64, 4, 512], P('rad', None, 'hel')
All inputs are finite; a program needn't handle non-finite values.
Results may differ from a plain program's by a relative error of at most 0.007.
Values may be sent and summed in bfloat16 or wider, within the bound.
A program may use at most 128 MiB of HBM per device.

v0:
```python
import jax
import jax.numpy as jnp
from jax import lax
from jax.sharding import PartitionSpec as P


def padded_2(cells, sides, width):
    for axis, dim in sides:
        count = lax.axis_size(axis)
        ends = count - 1
        head = lax.slice_in_dim(cells, 0, width, axis=dim)
        tail = lax.slice_in_dim(cells, cells.shape[dim] - width, cells.shape[dim], axis=dim)
        cells = jnp.concatenate(
            [
                lax.ppermute(tail, axis, [(i, (i + 1) % count) for i in range(ends)]),
                cells,
                lax.ppermute(head, axis, [((i + 1) % count, i) for i in range(ends)]),
            ],
            axis=dim,
        )
    return cells


def right_kinetic(packet, joined):
    width = joined.shape[0]
    flat = packet.reshape(-1, width)
    product = jnp.dot(flat, joined, preferred_element_type=jnp.float32)
    product = product.reshape(packet.shape[:-1] + (2 * width,))
    real_part = product[:, 0, ..., :width] - product[:, 1, ..., width:]
    imag_part = product[:, 0, ..., width:] + product[:, 1, ..., :width]
    return jnp.stack([real_part, imag_part], axis=1).astype(jnp.bfloat16)


def left_kinetic(columns, joined):
    width = joined.shape[0]
    flat = columns.reshape(width, -1)
    product = lax.dot_general(
        joined, flat, (((0,), (0,)), ((), ())), preferred_element_type=jnp.float32
    )
    product = product.reshape(2, width, 2, -1)
    real_part = product[0, :, 0] - product[1, :, 1]
    imag_part = product[0, :, 1] + product[1, :, 0]
    return jnp.stack([real_part, imag_part], axis=1).astype(jnp.bfloat16).reshape(columns.shape)


def per_device(packet, first_propagator, second_propagator, potential, coupling, radial_weight):
    blocks = packet.shape[2]
    joined_first = jnp.concatenate([first_propagator[0], first_propagator[1]], axis=1)
    joined_second = jnp.concatenate([second_propagator[0], second_propagator[1]], axis=1)
    half = right_kinetic(packet, joined_second)
    columns = lax.all_to_all(half, "rad", split_axis=4, concat_axis=0, tiled=True)
    propagated = left_kinetic(columns, joined_first)
    moved = lax.all_to_all(propagated, "rad", split_axis=0, concat_axis=4, tiled=True)
    cosine = jnp.cos(potential)[:, None, :, :]
    sine = jnp.sin(potential)[:, None, :, :]
    moved_float = moved.astype(jnp.float32)
    phased = jnp.stack(
        [
            moved_float[:, 0] * cosine + moved_float[:, 1] * sine,
            moved_float[:, 1] * cosine - moved_float[:, 0] * sine,
        ],
        axis=1,
    ).astype(jnp.bfloat16)
    kinetic = right_kinetic(phased, joined_second)
    padded = padded_2(kinetic, (("hel", 2),), 1)
    upper = padded[:, :, 2:].astype(jnp.float32)
    lower = padded[:, :, :-2].astype(jnp.float32)
    count = coupling.shape[0]
    helicities = jnp.arange(count, dtype=jnp.int32)
    couple_up = jnp.where(helicities[:, None] < count - 1, coupling, 0.0)
    couple_down = jnp.concatenate(
        [jnp.zeros((1, coupling.shape[1]), jnp.float32), coupling[:-1]], axis=0
    )
    block_start = lax.axis_index("hel") * blocks
    factor_up = lax.dynamic_slice_in_dim(couple_up, block_start, blocks, 0)[None, None, :, :, None]
    factor_down = lax.dynamic_slice_in_dim(couple_down, block_start, blocks, 0)[
        None, None, :, :, None
    ]
    mixing = factor_up * upper + factor_down * lower
    current = kinetic.astype(jnp.float32)
    weight = radial_weight[:, None, None, :]
    real_part = current[:, 0] + weight * mixing[:, 1]
    imag_part = current[:, 1] - weight * mixing[:, 0]
    return jnp.stack([real_part, imag_part], axis=1).astype(jnp.bfloat16)


def solution(mesh):
    return jax.shard_map(
        per_device,
        mesh=mesh,
        in_specs=(
            P("rad", None, "hel", None, None),
            P(),
            P(),
            P("rad", None, None),
            P(),
            P("rad", None),
        ),
        out_specs=P("rad", None, "hel", None, None),
        check_vma=False,
    )
```

profile of v0, /device:TPU:32, one launch (start us, length us, event | category | flops | bytes accessed | tf_op | source)
XLA Modules:
  0.0 288.9 jit_solution(7288215854024329579)
XLA Ops:
  4.1 7.2 %convolution_bitcast_fusion = f32[2048,1024]{0,1:T(8,128)} fusion(bf16[2048,512]{1,0:T(8,128)(2,1)} %reshape.76, bf16[512,512]{1,0:T(8,128)(2,1)S(1)} %get-tuple-element.22, bf16[512,512]{1,0:T(8,128)(2,1)S(1)} %get-tuple-element.21), kind=kOutput, calls=%fused_computation | convolution fusion | flops 2149580800 | bytes 11534336 | tf_op jit(solution)/shard_map/dot_general | solution.py:27
  11.3 9.3 %copy.80 = f32[2048,1024]{1,0:T(8,128)} copy(f32[2048,1024]{0,1:T(8,128)} %convolution_bitcast_fusion) | data formatting | bytes 16777216 | tf_op jit(solution)/shard_map/dot_general | solution.py:27
  20.6 9.8 %reshape.77 = f32[64,2,4,4,1024]{4,3,2,1,0:T(4,128)} reshape(f32[2048,1024]{1,0:T(8,128)} %copy.80) | data formatting | bytes 16777216 | tf_op jit(solution)/shard_map/reshape | solution.py:28
  30.4 4.4 %fusion.10 = (bf16[64,1,4,4,512]{4,3,2,1,0:T(4,128)(2,1)S(1)}, bf16[64,1,4,4,512]{4,3,2,1,0:T(4,128)(2,1)S(1)}) fusion(f32[64,2,4,4,1024]{4,3,2,1,0:T(4,128)} %reshape.77), kind=kLoop, calls=%fused_computation.30 | loop fusion | flops 2097152 | bytes 10485760 | tf_op jit(solution)/shard_map/convert.13
  36.1 6.2 %copy.81 = bf16[64,2,4,4,512]{0,3,2,1,4:T(4,128)(2,1)} copy(bf16[64,2,4,4,512]{4,3,2,1,0:T(4,128)(2,1)S(1)} %pad_maximum_fusion.5) | data formatting | bytes 4194304 | tf_op jit(solution)/shard_map/stack | solution.py:31
  42.3 7.5 %reshape.84 = bf16[16,2,32768]{2,1,0:T(2,128)(2,1)} reshape(bf16[512,2,4,4,64]{4,3,2,1,0:T(4,128)(2,1)} %bitcast.53) | data formatting | bytes 4194304
  49.8 10.3 %all-to-all-start = ((bf16[16,2,32768]{2,1,0:T(2,128)(2,1)}), bf16[16,2,32768]{2,1,0:T(2,128)(2,1)S(1)}, u32[]{:S(2)}, u32[]{:S(2)}) async-start(bf16[16,2,32768]{2,1,0:T(2,128)(2,1)} %reshape.84), calls=%async_computation | async-start | bytes 4194304 | tf_op jit(solution)/shard_map/all_to_all | solution.py:51
  65.3 6.4 %copy.79 = bf16[2048,1024]{1,0:T(8,128)(2,1)} copy(bf16[2048,1024]{0,1:T(8,128)(2,1)} %maximum_bitcast_fusion) | data formatting | bytes 8388608 | tf_op jit(solution)/shard_map/dot_general | solution.py:37
  71.7 40.2 %all-to-all-done = bf16[16,2,32768]{2,1,0:T(2,128)(2,1)S(1)} async-done(((bf16[16,2,32768]{2,1,0:T(2,128)(2,1)}), bf16[16,2,32768]{2,1,0:T(2,128)(2,1)S(1)}, u32[]{:S(2)}, u32[]{:S(2)}) %all-to-all-start) | async-done | bytes 2097184 | tf_op jit(solution)/shard_map/all_to_all | solution.py:51
  111.9 5.0 %reshape.85 = bf16[512,2,4,4,64]{4,3,2,1,0:T(4,128)(2,1)} reshape(bf16[16,2,32768]{2,1,0:T(2,128)(2,1)S(1)} %all-to-all-done) | data formatting | bytes 4194304
  116.9 3.8 %copy.82 = bf16[64,2,4,4,512]{0,4,3,2,1:T(8,128)(2,1)S(1)} copy(bf16[64,2,4,4,512]{0,3,2,1,4:T(4,128)(2,1)} %bitcast.54) | data formatting | bytes 4194304 | tf_op jit(solution)/shard_map/all_to_all | solution.py:51
  120.7 3.9 %copy.83 = bf16[16,64,2,4,4,32]{1,0,5,4,3,2:T(8,128)(2,1)} copy(bf16[16,64,2,4,4,32]{1,5,0,4,3,2:T(8,128)(2,1)S(1)} %bitcast.55) | data formatting | bytes 4194304 | tf_op jit(solution)/shard_map/all_to_all | solution.py:51
  124.6 5.5 %reshape.78 = bf16[1024,1024]{0,1:T(8,128)(2,1)S(1)} reshape(bf16[16,64,2,4,4,32]{1,0,5,4,3,2:T(8,128)(2,1)} %copy.83) | data formatting | bytes 4194304 | tf_op jit(solution)/shard_map/reshape | solution.py:36
  130.1 6.4 %fusion.22 = f32[2,1024,2,512]{1,3,2,0:T(8,128)S(1)} fusion(bf16[2,1024,1024,1]{2,1,3,0:T(8,128)(2,1)} %bitcast.56, bf16[2,512,1024,1]{2,1,0,3:T(8,128)(2,1)S(1)} %bitcast.59), kind=kOutput, calls=%fused_computation.56 | convolution fusion | flops 4294967296 | bytes 14680064 | tf_op jit(solution)/shard_map/dot_general | solution.py:37
  137.5 10.5 %copy.84 = bf16[1024,2,4,4,32]{4,3,2,1,0:T(4,128)(2,1)} copy(bf16[1024,2,4,4,32]{0,4,3,2,1:T(8,128)(2,1)S(1)} %pad_maximum_fusion.6) | data formatting | bytes 4194304 | tf_op jit(solution)/shard_map/stack | solution.py:43
  147.9 14.5 %reshape.86 = bf16[16,2,32768]{2,1,0:T(2,128)(2,1)} reshape(bf16[1024,2,4,4,32]{4,3,2,1,0:T(4,128)(2,1)} %copy.84) | data formatting | bytes 4194304
  162.4 5.7 %all-to-all-start.1 = ((bf16[16,2,32768]{2,1,0:T(2,128)(2,1)}), bf16[16,2,32768]{2,1,0:T(2,128)(2,1)S(1)}, u32[]{:S(2)}, u32[]{:S(2)}) async-start(bf16[16,2,32768]{2,1,0:T(2,128)(2,1)} %reshape.86), calls=%async_computation.1 | async-start | bytes 4194304 | tf_op jit(solution)/shard_map/all_to_all | solution.py:53
  170.4 50.4 %all-to-all-done.1 = bf16[16,2,32768]{2,1,0:T(2,128)(2,1)S(1)} async-done(((bf16[16,2,32768]{2,1,0:T(2,128)(2,1)}), bf16[16,2,32768]{2,1,0:T(2,128)(2,1)S(1)}, u32[]{:S(2)}, u32[]{:S(2)}) %all-to-all-start.1) | async-done | bytes 2097184 | tf_op jit(solution)/shard_map/all_to_all | solution.py:53
  220.8 8.7 %reshape.87 = bf16[1024,2,4,4,32]{4,3,2,1,0:T(4,128)(2,1)} reshape(bf16[16,2,32768]{2,1,0:T(2,128)(2,1)S(1)} %all-to-all-done.1) | data formatting | bytes 4194304
  229.5 10.8 %copy.85 = bf16[1024,2,4,4,32]{0,4,3,2,1:T(8,128)(2,1)S(1)} copy(bf16[1024,2,4,4,32]{4,3,2,1,0:T(4,128)(2,1)} %reshape.87) | data formatting | bytes 4194304 | tf_op jit(solution)/shard_map/all_to_all | solution.py:53
  240.4 4.5 %reshape.80 = f32[16,64,2,4,4,32]{1,0,5,4,3,2:T(8,128)} reshape(bf16[1024,2,4,4,32]{0,4,3,2,1:T(8,128)(2,1)S(1)} %copy.85) | data formatting | bytes 6291456 | tf_op jit(solution)/shard_map/convert_element_type | solution.py:56
  244.8 6.8 %copy.86 = f32[64,2,4,4,16,32]{0,5,4,3,2,1:T(8,128)S(1)} copy(f32[64,2,4,4,16,32]{0,4,5,3,2,1:T(8,128)} %bitcast.51) | data formatting | bytes 8388608 | tf_op jit(solution)/shard_map/convert_element_type | solution.py:56
  251.7 3.8 %fusion.20 = (f32[64,1,4,4,512]{0,4,3,2,1:T(8,128)}, f32[64,1,4,4,512]{0,4,3,2,1:T(8,128)}) fusion(f32[64,2,4,4,512]{0,4,3,2,1:T(8,128)S(1)} %bitcast.52), kind=kLoop, calls=%fused_computation.54 | loop fusion | bytes 8388608 | tf_op jit(solution)/shard_map/slice | solution.py:59
  277.8 5.8 %collective-permute-done.1 = bf16[64,2,1,4,512]{4,0,3,2,1:T(8,128)(2,1)S(1)} collective-permute-done((bf16[64,2,1,4,512]{4,0,3,2,1:T(8,128)(2,1)}, bf16[64,2,1,4,512]{4,0,3,2,1:T(8,128)(2,1)S(1)}, u32[]{:S(2)}, u32[]{:S(2)}) %collective-permute-start.1) | collective-permute-done | bytes 524320 | tf_op jit(solution)/shard_map/ppermute | solution.py:15
  (45 shorter events, 41.2 us)
Async XLA Ops:
  0.0 1.9 copy-start
  1.9 2.2 copy-start.2
  1.9 2.2 copy-start.4
  49.8 62.0 %all-to-all-start = ((bf16[16,2,32768]{2,1,0:T(2,128)(2,1)}), bf16[16,2,32768]{2,1,0:T(2,128)(2,1)S(1)}, u32[]{:S(2)}, u32[]{:S(2)}) async-start(bf16[16,2,32768]{2,1,0:T(2,128)(2,1)} %reshape.84), calls=%async_computation | async-start | bytes 4194304 | tf_op jit(solution)/shard_map/all_to_all | solution.py:51
  162.4 5.7 %copy-start.1 = (f32[64,4,512]{2,1,0:T(4,128)S(1)}, f32[64,4,512]{2,1,0:T(4,128)}, u32[]{:S(2)}) copy-start(f32[64,4,512]{2,1,0:T(4,128)} %param.9) | copy-start | bytes 1572868
  162.4 58.4 %all-to-all-start.1 = ((bf16[16,2,32768]{2,1,0:T(2,128)(2,1)}), bf16[16,2,32768]{2,1,0:T(2,128)(2,1)S(1)}, u32[]{:S(2)}, u32[]{:S(2)}) async-start(bf16[16,2,32768]{2,1,0:T(2,128)(2,1)} %reshape.86), calls=%async_computation.1 | async-start | bytes 4194304 | tf_op jit(solution)/shard_map/all_to_all | solution.py:53
  262.1 2.4 copy-start.3
  262.1 2.5 copy-start.5
  267.8 5.7 %copy-start.7 = (f32[64,4]{0,1:T(4,128)S(1)}, f32[64,4]{0,1:T(4,128)}, u32[]{:S(2)}) copy-start(f32[64,4]{0,1:T(4,128)} %param.10) | copy-start | bytes 3076
  268.8 8.9 %collective-permute-start = (bf16[64,2,1,4,512]{4,0,3,2,1:T(8,128)(2,1)}, bf16[64,2,1,4,512]{4,0,3,2,1:T(8,128)(2,1)S(1)}, u32[]{:S(2)}, u32[]{:S(2)}) collective-permute-start(bf16[64,2,1,4,512]{4,0,3,2,1:T(8,128)(2,1)} %get-tuple-element.19), channel_id=1, source_target_pairs={{16,0},{32,16},{48,32},{64,48},{80,64},{96,80},{112,96},{128,112},... | collective-permute-start | bytes 1572872 | tf_op jit(solution)/shard_map/ppermute | solution.py:17
  270.8 12.8 %collective-permute-start.1 = (bf16[64,2,1,4,512]{4,0,3,2,1:T(8,128)(2,1)}, bf16[64,2,1,4,512]{4,0,3,2,1:T(8,128)(2,1)S(1)}, u32[]{:S(2)}, u32[]{:S(2)}) collective-permute-start(bf16[64,2,1,4,512]{4,0,3,2,1:T(8,128)(2,1)} %get-tuple-element.20), channel_id=1, source_target_pairs={{0,16},{16,32},{32,48},{48,64},{64,80},{80,96},{96,112},{112,128},... | collective-permute-start | bytes 1572872 | tf_op jit(solution)/shard_map/ppermute | solution.py:15
  274.0 10.5 %copy-start.6 = (f32[64,512]{1,0:T(8,128)S(1)}, f32[64,512]{1,0:T(8,128)}, u32[]{:S(2)}) copy-start(f32[64,512]{1,0:T(8,128)} %param.11) | copy-start | bytes 393220
where the time goes:
time: 291 us; the launch traced here: 289 us
  local copies, waits for them, and re-layouts  136 us (47%)
  waiting for transfers between devices  100 us (34%)
  starting transfers between devices  20.6 us (7%)
  other arithmetic  16.1 us (6%)
  matrix products  15.9 us (5%)
    all_to_all x1, waiting for transfers between devices, per_device(): lax.all_to_all(propagated, 'rad', split_axis=0, concat_axis=4, tiled=True)  50.4 us
    unnamed x22, local copies, waits for them, and re-layouts  42.9 us
    all_to_all x1, waiting for transfers between devices, per_device(): lax.all_to_all(half, 'rad', split_axis=4, concat_axis=0, tiled=True)  40.2 us
    convert_element_type x2, local copies, waits for them, and re-layouts, per_device(): moved_float = moved.astype(jnp.float32)  11.3 us
    all_to_all x1, local copies, waits for them, and re-layouts, per_device(): lax.all_to_all(propagated, 'rad', split_axis=0, concat_axis=4, tiled=True)  10.8 us
    another operation x1, local copies, waits for them, and re-layouts, left_kinetic(): jnp.stack([real_part, imag_part], axis=1).astype(jnp.bfloat16)  10.5 us
    all_to_all x1, starting transfers between devices, per_device(): lax.all_to_all(half, 'rad', split_axis=4, concat_axis=0, tiled=True)  10.3 us
    reshape x1, local copies, waits for them, and re-layouts, right_kinetic(): product = product.reshape(packet.shape[:-1] + (2 * width,))  9.78 us
  transfers between devices with their start and end apart: 4, of which 4 were waited for; matrix products, arithmetic and copies ran while one was open for 5% of the time, Pallas kernels for 0%

commit v1 on v0

v1 whole, which is shorter than its diff:
```python
import functools

import jax
import jax.numpy as jnp
from jax import lax
from jax.experimental import pallas as pl
from jax.experimental.pallas import tpu as pltpu
from jax.sharding import PartitionSpec as P

MESH = pl.DeviceIdType.MESH
BF16 = jnp.bfloat16
F32 = jnp.float32


def kernel(
    n_hel,
    n_rad,
    coup,
    pk,
    p1,
    p2,
    pot,
    rw,
    out,
    pkv,
    xs,
    p2v,
    pbig,
    p1v,
    p1t,
    potv,
    cosv,
    sinv,
    wv,
    fscr,
    hs,
    cols,
    ps,
    mv,
    ph,
    kin,
    outv,
    load_sem,
    pk_sem,
    out_sem,
    send1,
    recv1,
    send2,
    recv2,
    hsend,
    hrecv,
):
    kk = pkv.shape[0]
    h = lax.axis_index("hel")
    r = lax.axis_index("rad")
    partner = lax.rem(h + n_hel // 2, n_hel)
    zh, y = r // 4, lax.rem(r, 4)

    def order(i):
        return lax.rem(3 * i, 4)

    def peer(i):
        return lax.rem(zh + i, 4) * 4 + lax.rem(y + i // 4, 4)

    def load_packet(i):
        k = order(i)
        return [
            pltpu.make_async_copy(pk.at[:, c, k], pkv.at[k, c], pk_sem.at[i, c])
            for c in range(2)
        ]

    load_p2 = pltpu.make_async_copy(p2, p2v, load_sem.at[0])
    load_p1 = pltpu.make_async_copy(p1, p1v, load_sem.at[1])
    load_pot = pltpu.make_async_copy(pot, potv, load_sem.at[2])
    load_w = pltpu.make_async_copy(rw, wv, load_sem.at[3])
    load_p2.start()
    for i in range(kk):
        for copy in load_packet(i):
            copy.start()
    load_p1.start()
    load_pot.start()
    load_w.start()

    barrier = pltpu.get_barrier_semaphore()

    def greet(i, carry):
        pl.semaphore_signal(
            barrier, inc=1, device_id=(partner, peer(i)), device_id_type=MESH
        )
        return carry

    lax.fori_loop(0, n_rad, greet, 0)

    @pl.when(h > 0)
    def _():
        pl.semaphore_signal(barrier, inc=1, device_id=(h - 1, r), device_id_type=MESH)

    @pl.when(h < n_hel - 1)
    def _():
        pl.semaphore_signal(barrier, inc=1, device_id=(h + 1, r), device_id_type=MESH)

    load_p2.wait()
    for s in range(4):
        lanes = slice(s * 128, (s + 1) * 128)
        real, imag = p2v[0, :, lanes], p2v[1, :, lanes]
        pbig[:512, s * 256 : s * 256 + 128] = real
        pbig[:512, s * 256 + 128 : (s + 1) * 256] = imag
        pbig[512:, s * 256 : s * 256 + 128] = -imag
        pbig[512:, s * 256 + 128 : (s + 1) * 256] = real

    neighbours = jnp.where(h > 0, 1, 0) + jnp.where(h < n_hel - 1, 1, 0)
    pl.semaphore_wait(barrier, n_rad + neighbours)

    def first(i, carry):
        k = order(i)
        for copy in load_packet(i):
            copy.wait()
        for c in range(2):
            xs[:, c * 512 : (c + 1) * 512] = pkv[k, c].reshape(256, 512)
        for s in range(4):
            part = jnp.dot(
                xs[...],
                pbig[:, s * 256 : (s + 1) * 256],
                preferred_element_type=F32,
            )
            fscr[2 * s] = part[:, :128]
            fscr[2 * s + 1] = part[:, 128:]
        for j in range(4):
            for s in range(4):
                for c in range(2):
                    rows = fscr.at[2 * s + c][pl.ds(j, 64, stride=4), :]
                    hs[k, j * 4 + s, :, c * 128 : (c + 1) * 128] = rows.astype(BF16)

        def send(n, carry):
            p = peer(n)
            pltpu.make_async_remote_copy(
                src_ref=hs.at[k, p],
                dst_ref=cols.at[k, r],
                send_sem=send1.at[k],
                recv_sem=recv1.at[k],
                device_id=(partner, p),
                device_id_type=MESH,
            ).start()
            return carry

        lax.fori_loop(0, n_rad, send, 0)
        return carry

    lax.fori_loop(0, kk, first, 0)

    load_p1.wait()

    def flip(n, carry):
        rows = pl.ds(pl.multiple_of(n * 128, 128), 128)
        for c in range(2):
            p1t[c, rows, :] = p1v[c, :, rows].T
        return carry

    lax.fori_loop(0, 8, flip, 0)
    load_pot.wait()
    for s in range(4):
        fscr[s] = potv[:, :, s * 128 : (s + 1) * 128].reshape(256, 128)

    def phases(s, carry):
        for j in range(4):
            angle = fscr.at[s][pl.ds(j, 64, stride=4), :]
            cosv[j, s] = jnp.cos(angle)
            sinv[j, s] = jnp.sin(angle)
        return carry

    lax.fori_loop(0, 4, phases, 0)
    load_w.wait()

    def whole(src, dst, sems, i):
        return pltpu.make_async_remote_copy(
            src_ref=src.at[i],
            dst_ref=dst.at[i],
            send_sem=sems[0].at[i],
            recv_sem=sems[1].at[i],
            device_id=(partner, r),
            device_id_type=MESH,
        )

    def second(i, carry):
        k = order(i)
        whole(hs, cols, (send1, recv1), k).wait_recv()

        def block(n, carry):
            rows = pl.ds(pl.multiple_of(n * 256, 256), 256)
            u = cols[k].reshape(1024, 256)
            a = jnp.dot(p1t[0, rows, :], u, preferred_element_type=F32)
            b = jnp.dot(p1t[1, rows, :], u, preferred_element_type=F32)
            real = a[:, :128] - b[:, 128:]
            imag = a[:, 128:] + b[:, :128]
            four = pl.ds(n * 4, 4)
            ps[k, four, :, :128] = real.astype(BF16).reshape(4, 64, 128)
            ps[k, four, :, 128:] = imag.astype(BF16).reshape(4, 64, 128)
            return carry

        lax.fori_loop(0, 4, block, 0)

        def send(n, carry):
            p = peer(n)
            pltpu.make_async_remote_copy(
                src_ref=ps.at[k, p],
                dst_ref=mv.at[k, r],
                send_sem=send2.at[k],
                recv_sem=recv2.at[k],
                device_id=(partner, p),
                device_id_type=MESH,
            ).start()
            return carry

        lax.fori_loop(0, n_rad, send, 0)
        return carry

    lax.fori_loop(0, kk, second, 0)

    @pl.when(h == 0)
    def _():
        kin[0] = jnp.zeros_like(kin[0])

    @pl.when(h == n_hel - 1)
    def _():
        kin[kk + 1] = jnp.zeros_like(kin[kk + 1])

    def halo(k):
        low = k == 0
        return pltpu.make_async_remote_copy(
            src_ref=kin.at[1 if low else kk],
            dst_ref=kin.at[kk + 1 if low else 0],
            send_sem=hsend.at[0 if low else 1],
            recv_sem=hrecv.at[0 if low else 1],
            device_id=(h - 1 if low else h + 1, r),
            device_id_type=MESH,
        )

    def mix(k):
        g = h * kk + k
        last = n_hel * kk - 1
        for j in range(4):
            up = jnp.where(g < last, coup[g, j], 0.0)
            down = jnp.where(g > 0, coup[jnp.maximum(g - 1, 0), j], 0.0)
            rows = slice(j * 64, (j + 1) * 64)
            for s in range(4):
                re = slice(s * 256, s * 256 + 128)
                im = slice(s * 256 + 128, (s + 1) * 256)
                w = wv[:, s * 128 : (s + 1) * 128]
                mixed_im = up * kin[k + 2, rows, im].astype(F32) + down * kin[
                    k, rows, im
                ].astype(F32)
                mixed_re = up * kin[k + 2, rows, re].astype(F32) + down * kin[
                    k, rows, re
                ].astype(F32)
                place = pl.ds(j, 64, stride=4)
                fscr.at[s][place, :] = kin[k + 1, rows, re].astype(F32) + w * mixed_im
                fscr.at[4 + s][place, :] = (
                    kin[k + 1, rows, im].astype(F32) - w * mixed_re
                )
        for c in range(2):
            for s in range(4):
                outv[k, c, :, :, s * 128 : (s + 1) * 128] = (
                    fscr[4 * c + s].astype(BF16).reshape(64, 4, 128)
                )
        for c in range(2):
            pltpu.make_async_copy(
                outv.at[k, c], out.at[:, c, k], out_sem.at[k, c]
            ).start()

    def third(i, carry):
        k = order(i)
        whole(ps, mv, (send2, recv2), k).wait_recv()
        for j in range(4):
            rows = slice(j * 64, (j + 1) * 64)
            for s in range(4):
                re = mv[k, j * 4 + s, :, :128].astype(F32)
                im = mv[k, j * 4 + s, :, 128:].astype(F32)
                c, sn = cosv[j, s], sinv[j, s]
                ph[rows, s * 128 : (s + 1) * 128] = (re * c + im * sn).astype(BF16)
                ph[rows, 512 + s * 128 : 512 + (s + 1) * 128] = (
                    im * c - re * sn
                ).astype(BF16)
        for s in range(4):
            lanes = slice(s * 256, (s + 1) * 256)
            kin[k + 1, :, lanes] = jnp.dot(
                ph[...], pbig[:, lanes], preferred_element_type=F32
            ).astype(BF16)

        @pl.when((i == 0) & (h > 0))
        def _():
            halo(0).start()

        @pl.when((i == 1) & (h < n_hel - 1))
        def _():
            halo(kk - 1).start()

        @pl.when(i == 2)
        def _():
            @pl.when(h < n_hel - 1)
            def _():
                halo(0).wait_recv()

            mix(kk - 1)

        return carry

    lax.fori_loop(0, kk, third, 0)

    @pl.when(h > 0)
    def _():
        halo(kk - 1).wait_recv()

    def rest(k, carry):
        mix(k)
        return carry

    lax.fori_loop(0, kk - 1, rest, 0)

    def drain(k, carry):
        whole(hs, cols, (send1, recv1), k).wait_send()
        whole(ps, mv, (send2, recv2), k).wait_send()
        for c in range(2):
            pltpu.make_async_copy(outv.at[k, c], out.at[:, c, k], out_sem.at[k, c]).wait()
        return carry

    lax.fori_loop(0, kk, drain, 0)

    @pl.when(h > 0)
    def _():
        halo(0).wait_send()

    @pl.when(h < n_hel - 1)
    def _():
        halo(kk - 1).wait_send()


def solution(mesh):
    n_hel, n_rad = mesh.shape["hel"], mesh.shape["rad"]

    def per_device(packet, first, second, potential, coupling, weight):
        hbm = pl.BlockSpec(memory_space=pl.ANY)
        dma = pltpu.SemaphoreType.DMA
        return pl.pallas_call(
            functools.partial(kernel, n_hel, n_rad),
            out_shape=jax.ShapeDtypeStruct(packet.shape, BF16),
            in_specs=[pl.BlockSpec(memory_space=pltpu.SMEM)] + [hbm] * 5,
            out_specs=hbm,
            scratch_shapes=[
                pltpu.VMEM((4, 2, 64, 4, 512), BF16),
                pltpu.VMEM((256, 1024), BF16),
                pltpu.VMEM((2, 512, 512), BF16),
                pltpu.VMEM((1024, 1024), BF16),
                pltpu.VMEM((2, 1024, 1024), BF16),
                pltpu.VMEM((2, 1024, 1024), BF16),
                pltpu.VMEM((64, 4, 512), F32),
                pltpu.VMEM((4, 4, 64, 128), F32),
                pltpu.VMEM((4, 4, 64, 128), F32),
                pltpu.VMEM((64, 512), F32),
                pltpu.VMEM((8, 256, 128), F32),
                pltpu.VMEM((4, 16, 64, 256), BF16),
                pltpu.VMEM((4, 16, 64, 256), BF16),
                pltpu.VMEM((4, 16, 64, 256), BF16),
                pltpu.VMEM((4, 16, 64, 256), BF16),
                pltpu.VMEM((256, 1024), BF16),
                pltpu.VMEM((6, 256, 1024), BF16),
                pltpu.VMEM((4, 2, 64, 4, 512), BF16),
                dma((4,)),
                dma((4, 2)),
                dma((4, 2)),
                dma((4,)),
                dma((4,)),
                dma((4,)),
                dma((4,)),
                dma((2,)),
                dma((2,)),
            ],
            compiler_params=pltpu.CompilerParams(
                collective_id=0, has_side_effects=True
            ),
        )(coupling, packet, first, second, potential, weight)

    return jax.shard_map(
        per_device,
        mesh=mesh,
        in_specs=(
            P("rad", None, "hel", None, None),
            P(),
            P(),
            P("rad", None, None),
            P(),
            P("rad", None),
        ),
        out_specs=P("rad", None, "hel", None, None),
        check_vma=False,
    )
```

time: 291 us -> 119 us (0.41)
  local copies, waits for them, and re-layouts: 136 us -> 6.02 us
  Pallas kernels: 0 us -> 112 us
  waiting for transfers between devices: 100 us -> 0 us
  starting transfers between devices: 20.6 us -> 0 us
  other arithmetic: 16.1 us -> 0 us
  matrix products: 15.9 us -> 0 us
    pallas_call x0 -> x1, Pallas kernels: none -> 112 us  [per_device(): pl.pallas_call(functools.partial(kernel, n_hel, n_rad), out_shape=jax.Sha...]
    all_to_all x2 -> x0, waiting for transfers between devices: 90.6 us -> none  [the longest x1 50.4 us: per_device(): lax.all_to_all(propagated, 'rad', split_axis=0, concat_axis=4, tiled=True)]
    unnamed x22 -> x2, local copies, waits for them, and re-layouts: 42.9 us -> 6.02 us
    another operation x3 -> x0, local copies, waits for them, and re-layouts: 19.6 us -> none  [the longest x1 10.5 us: left_kinetic(): jnp.stack([real_part, imag_part], axis=1).astype(jnp.bfloat16)]
    all_to_all x3 -> x0, local copies, waits for them, and re-layouts: 18.6 us -> none  [the longest x1 10.8 us: per_device(): lax.all_to_all(propagated, 'rad', split_axis=0, concat_axis=4, tiled=True)]
    reshape x3 -> x0, local copies, waits for them, and re-layouts: 17.4 us -> none  [the longest x1 9.78 us: right_kinetic(): product = product.reshape(packet.shape[:-1] + (2 * width,))]
    all_to_all x2 -> x0, starting transfers between devices: 16 us -> none  [the longest x1 10.3 us: per_device(): lax.all_to_all(half, 'rad', split_axis=4, concat_axis=0, tiled=True)]
    dot_general x3 -> x0, matrix products: 15.9 us -> none  [the longest x2 9.56 us: right_kinetic(): product = jnp.dot(flat, joined, preferred_element_type=jnp.float32)]
  transfers between devices with their start and end apart: 4 -> 0, of which waited for: 4 -> 0; matrix products, arithmetic and copies ran while one was open for 5% -> 0% of each run, Pallas kernels for 0% -> 0%
where the time goes in v1:
time: 119 us
  Pallas kernels  112 us (94%)
  local copies, waits for them, and re-layouts  6.02 us (5%)
    pallas_call x1, Pallas kernels, per_device(): pl.pallas_call(functools.partial(kernel, n_hel, n_rad), out_shape=jax.Sha...  112 us
    unnamed x2, local copies, waits for them, and re-layouts  6.02 us

profile of v1, /device:TPU:32, one launch (start us, length us, event | category | flops | bytes accessed | tf_op | source)
XLA Modules:
  0.0 118.5 jit_solution(16267956241946738512)
XLA Ops:
  0.0 1.4 %copy.7.coup = f32[64,4]{1,0:T(8,128)} copy(f32[64,4]{0,1:T(4,128)} %param.10) | data formatting | bytes 2048 | tf_op args[4]
  1.4 112.5 %shard_map.64 = bf16[64,2,4,4,512]{4,3,2,1,0:T(4,128)(2,1)} custom-call(f32[64,4]{1,0:T(8,128)} %copy.7.coup, bf16[64,2,4,4,512]{4,3,2,1,0:T(4,128)(2,1)} %pk.1, bf16[2,1024,1024]{2,1,0:T(8,128)(2,1)} %p1.1, bf16[2,512,512]{2,1,0:T(8,128)(2,1)} %p2.1, f32[64,4,512]{2,1,0:T(4,128)} %pot.1, f32[64,512]{1,0:T(8,128)} %rw.1), custom_call_target="tpu_custom_call" | custom-call | tf_op jit(solution)/shard_map/pallas_call | solution.py:343
  113.9 4.6 %copy.9 = bf16[64,2,4,4,512]{4,3,2,1,0:T(4,128)(2,1)} copy(bf16[64,2,4,4,512]{4,3,2,1,0:T(4,128)(2,1)} %shard_map.64) | data formatting | bytes 4194304

commit v2 on v1

v2 whole, which is shorter than its diff:
```python
import functools

import jax
import jax.numpy as jnp
from jax import lax
from jax.experimental import pallas as pl
from jax.experimental.pallas import tpu as pltpu
from jax.sharding import PartitionSpec as P

MESH = pl.DeviceIdType.MESH
BF16 = jnp.bfloat16
F32 = jnp.float32


def kernel(
    n_hel,
    n_rad,
    coup_hbm,
    pk,
    p1,
    p2,
    pot,
    rw,
    outv,
    pkv,
    xs,
    p2v,
    pbig,
    p1v,
    p1t,
    potv,
    cosv,
    sinv,
    wv,
    coup,
    fscr,
    hs,
    cols,
    ps,
    mv,
    ph,
    kin,
    relay,
    load_sem,
    pk_sem,
    send1,
    recv1,
    send2,
    recv2,
    hsend,
    hrecv,
    rsend,
    rrecv,
):
    kk = pkv.shape[0]
    h = lax.axis_index("hel")
    r = lax.axis_index("rad")
    middle = n_hel // 2
    partner = lax.rem(h + middle, n_hel)
    zh, y = r // 4, lax.rem(r, 4)
    z_lo = h // middle
    last_k = 1

    def order(i):
        return lax.rem(3 * i, 4)

    def peer(i):
        b = i // 4
        dy = jnp.where(b == 0, 2, jnp.where(b == 3, 0, 2 * b - 1))
        return lax.rem(zh + lax.rem(i, 4) + 1 + z_lo, 4) * 4 + lax.rem(y + dy, 4)

    is_low, is_high = h == middle - 1, h == middle
    carries_down = (h > middle + 1) & (lax.rem(h, 2) == 1)
    carries_up = (h < middle - 2) & (lax.rem(h, 2) == 1)

    barrier = pltpu.get_barrier_semaphore()

    def greet_one(target, rad):
        pl.semaphore_signal(
            barrier, inc=1, device_id=(target, rad), device_id_type=MESH
        )

    def greet(i, carry):
        greet_one(partner, peer(i))
        return carry

    lax.fori_loop(0, n_rad, greet, 0)

    @pl.when(h > 0)
    def _():
        greet_one(h - 1, r)

    @pl.when(h < n_hel - 1)
    def _():
        greet_one(h + 1, r)

    @pl.when(carries_down)
    def _():
        greet_one(middle, r)

    @pl.when(carries_up)
    def _():
        greet_one(middle - 1, r)

    @pl.when(is_low)
    def _():
        for q in range(1, 4):
            greet_one(middle + 2 * q + 1, r)

    @pl.when(is_high)
    def _():
        for q in range(3):
            greet_one(2 * q + 1, r)

    greeted = n_rad + jnp.where(h > 0, 1, 0) + jnp.where(h < n_hel - 1, 1, 0)
    greeted += jnp.where(is_low | is_high, 3, 0)
    greeted += jnp.where(carries_down | carries_up, 1, 0)

    def load_packet(i):
        k = order(i)
        return [
            pltpu.make_async_copy(pk.at[:, c, k], pkv.at[k, c], pk_sem.at[i, c])
            for c in range(2)
        ]

    load_p2 = pltpu.make_async_copy(p2, p2v, load_sem.at[0])
    load_p1 = pltpu.make_async_copy(p1, p1v, load_sem.at[1])
    load_pot = pltpu.make_async_copy(pot, potv, load_sem.at[2])
    load_w = pltpu.make_async_copy(rw, wv, load_sem.at[3])
    load_coup = pltpu.make_async_copy(coup_hbm, coup, load_sem.at[4])
    load_p2.start()
    for i in range(kk):
        for copy in load_packet(i):
            copy.start()
    load_p1.start()
    load_pot.start()
    load_w.start()
    load_coup.start()

    load_p2.wait()
    for s in range(4):
        lanes = slice(s * 128, (s + 1) * 128)
        real, imag = p2v[0, :, lanes], p2v[1, :, lanes]
        pbig[:512, s * 256 : s * 256 + 128] = real
        pbig[:512, s * 256 + 128 : (s + 1) * 256] = imag
        pbig[512:, s * 256 : s * 256 + 128] = -imag
        pbig[512:, s * 256 + 128 : (s + 1) * 256] = real

    def first(i, carry):
        k = order(i)
        for copy in load_packet(i):
            copy.wait()
        for c in range(2):
            xs[:, c * 512 : (c + 1) * 512] = pkv[k, c].reshape(256, 512)
        for s in range(4):
            part = jnp.dot(
                xs[...],
                pbig[:, s * 256 : (s + 1) * 256],
                preferred_element_type=F32,
            )
            fscr[2 * s] = part[:, :128]
            fscr[2 * s + 1] = part[:, 128:]
        for j in range(4):
            for s in range(4):
                for c in range(2):
                    rows = fscr.at[2 * s + c][pl.ds(j, 64, stride=4), :]
                    hs[k, j * 4 + s, :, c * 128 : (c + 1) * 128] = rows.astype(BF16)

        @pl.when(i == 0)
        def _():
            pl.semaphore_wait(barrier, greeted)

        def send(n, carry):
            p = peer(n)
            pltpu.make_async_remote_copy(
                src_ref=hs.at[k, p],
                dst_ref=cols.at[k, r],
                send_sem=send1.at[k],
                recv_sem=recv1.at[k],
                device_id=(partner, p),
                device_id_type=MESH,
            ).start()
            return carry

        lax.fori_loop(0, n_rad, send, 0)
        return carry

    lax.fori_loop(0, kk, first, 0)

    load_p1.wait()

    def flip(n, carry):
        rows = pl.ds(pl.multiple_of(n * 128, 128), 128)
        for c in range(2):
            p1t[c, rows, :] = p1v[c, :, rows].T
        return carry

    lax.fori_loop(0, 8, flip, 0)
    load_pot.wait()
    for s in range(4):
        fscr[s] = potv[:, :, s * 128 : (s + 1) * 128].reshape(256, 128)

    def phases(s, carry):
        for j in range(4):
            angle = fscr.at[s][pl.ds(j, 64, stride=4), :]
            cosv[j, s] = jnp.cos(angle)
            sinv[j, s] = jnp.sin(angle)
        return carry

    lax.fori_loop(0, 4, phases, 0)
    load_w.wait()
    load_coup.wait()

    def whole(src, dst, send_sem, recv_sem):
        return pltpu.make_async_remote_copy(
            src_ref=src,
            dst_ref=dst,
            send_sem=send_sem,
            recv_sem=recv_sem,
            device_id=(partner, r),
            device_id_type=MESH,
        )

    def all_first(k):
        return whole(hs.at[k], cols.at[k], send1.at[k], recv1.at[k])

    def all_second(k, base, rows, n):
        part = pl.ds(base, rows)
        return whole(
            ps.at[k, :, part], mv.at[k, :, part], send2.at[n], recv2.at[n]
        )

    def left(k):
        all_first(k).wait_recv()

        def block(n, carry):
            rows = pl.ds(pl.multiple_of(n * 256, 256), 256)
            u = cols[k].reshape(1024, 256)
            a = jnp.dot(p1t[0, rows, :], u, preferred_element_type=F32)
            b = jnp.dot(p1t[1, rows, :], u, preferred_element_type=F32)
            real = a[:, :128] - b[:, 128:]
            imag = a[:, 128:] + b[:, :128]
            four = pl.ds(n * 4, 4)
            ps[k, four, :, :128] = real.astype(BF16).reshape(4, 64, 128)
            ps[k, four, :, 128:] = imag.astype(BF16).reshape(4, 64, 128)
            return carry

        lax.fori_loop(0, 4, block, 0)

    def send_back(k, base, rows, n_sem):
        part = pl.ds(base, rows)

        def send(n, carry):
            p = peer(n)
            pltpu.make_async_remote_copy(
                src_ref=ps.at[k, p, part],
                dst_ref=mv.at[k, r, part],
                send_sem=send2.at[n_sem],
                recv_sem=recv2.at[n_sem],
                device_id=(partner, p),
                device_id_type=MESH,
            ).start()
            return carry

        lax.fori_loop(0, n_rad, send, 0)

    def second(i, carry):
        k = order(i)
        left(k)

        @pl.when(i < kk - 1)
        def _():
            send_back(k, 0, 64, i)

        @pl.when(i == kk - 1)
        def _():
            def part(n, carry):
                send_back(k, pl.multiple_of(n * 32, 32), 32, kk - 1 + n)
                return carry

            lax.fori_loop(0, 2, part, 0)

        return carry

    lax.fori_loop(0, kk, second, 0)

    @pl.when(h == 0)
    def _():
        kin[0] = jnp.zeros_like(kin[0])

    @pl.when(h == n_hel - 1)
    def _():
        kin[kk + 1] = jnp.zeros_like(kin[kk + 1])

    def ends(low):
        return (1, kk + 1, 0) if low else (kk, 0, 1)

    def halo(low):
        own, there, n = ends(low)
        return pltpu.make_async_remote_copy(
            src_ref=kin.at[own],
            dst_ref=kin.at[there],
            send_sem=hsend.at[n],
            recv_sem=hrecv.at[n],
            device_id=(h - 1 if low else h + 1, r),
            device_id_type=MESH,
        )

    def quarter(low, q, target, by_helper):
        own, there, n = ends(low)
        rows = pl.ds(q * 64, 64)
        return pltpu.make_async_remote_copy(
            src_ref=kin.at[own, rows],
            dst_ref=relay if by_helper else kin.at[there, rows],
            send_sem=hsend.at[n],
            recv_sem=rrecv if by_helper else hrecv.at[n],
            device_id=(target, r),
            device_id_type=MESH,
        )

    def hand_on(low):
        own, there, n = ends(low)
        q = (h - middle - 1) // 2 if low else (h - 1) // 2
        rows = pl.ds(pl.multiple_of(q * 64, 64), 64)
        return pltpu.make_async_remote_copy(
            src_ref=relay,
            dst_ref=kin.at[there, rows],
            send_sem=rsend,
            recv_sem=hrecv.at[n],
            device_id=(middle - 1 if low else middle, r),
            device_id_type=MESH,
        )

    def arrived_at_helper(low):
        return quarter(low, 0, partner, True)

    def mix(k, base, rows):
        g = h * kk + k
        last = n_hel * kk - 1
        for j in range(4):
            up = jnp.where(g < last, coup[j, g], 0.0)
            down = jnp.where(g > 0, coup[j, jnp.maximum(g - 1, 0)], 0.0)
            part = pl.ds(j * 64 + base, rows)
            for s in range(4):
                re = slice(s * 256, s * 256 + 128)
                im = slice(s * 256 + 128, (s + 1) * 256)
                w = wv[pl.ds(base, rows), s * 128 : (s + 1) * 128]
                mixed_im = up * kin[k + 2, part, im].astype(F32) + down * kin[
                    k, part, im
                ].astype(F32)
                mixed_re = up * kin[k + 2, part, re].astype(F32) + down * kin[
                    k, part, re
                ].astype(F32)
                place = pl.ds(j, rows, stride=4)
                fscr.at[s][place, :] = kin[k + 1, part, re].astype(F32) + w * mixed_im
                fscr.at[4 + s][place, :] = (
                    kin[k + 1, part, im].astype(F32) - w * mixed_re
                )
        for c in range(2):
            for s in range(4):
                outv[pl.ds(base, rows), c, k, :, s * 128 : (s + 1) * 128] = (
                    fscr[4 * c + s, : 4 * rows].astype(BF16).reshape(rows, 4, 128)
                )

    def finish(k, base, rows):
        part = pl.ds(base, rows)
        for j in range(4):
            place = slice(j * rows, (j + 1) * rows)
            for s in range(4):
                re = mv[k, j * 4 + s, part, :128].astype(F32)
                im = mv[k, j * 4 + s, part, 128:].astype(F32)
                c, sn = cosv[j, s, part], sinv[j, s, part]
                ph[place, s * 128 : (s + 1) * 128] = (re * c + im * sn).astype(BF16)
                ph[place, 512 + s * 128 : 512 + (s + 1) * 128] = (
                    im * c - re * sn
                ).astype(BF16)
        for s in range(4):
            lanes = slice(s * 256, (s + 1) * 256)
            result = jnp.dot(
                ph[: 4 * rows], pbig[:, lanes], preferred_element_type=F32
            ).astype(BF16)
            for j in range(4):
                kin[k + 1, pl.ds(j * 64 + base, rows), lanes] = result[
                    j * rows : (j + 1) * rows
                ]

    def third(i, carry):
        k = order(i)
        all_second(k, 0, 64, i).wait_recv()
        finish(k, 0, 64)

        @pl.when((i == 0) & (h > 0) & (h != middle))
        def _():
            halo(True).start()

        @pl.when((i == 1) & (h < n_hel - 1) & (h != middle - 1))
        def _():
            halo(False).start()

        @pl.when((i == 0) & is_high)
        def _():
            for q in range(1, 4):
                quarter(True, q, middle + 2 * q + 1, True).start()
            quarter(True, 0, middle - 1, False).start()

        @pl.when((i == 1) & is_low)
        def _():
            for q in range(3):
                quarter(False, q, 2 * q + 1, True).start()
            quarter(False, 3, middle, False).start()

        @pl.when((i == 1) & carries_down)
        def _():
            arrived_at_helper(True).wait_recv()
            hand_on(True).start()

        @pl.when((i == 2) & carries_up)
        def _():
            arrived_at_helper(False).wait_recv()
            hand_on(False).start()

        @pl.when((i == 2) & (h != middle - 1))
        def _():
            @pl.when(h < n_hel - 1)
            def _():
                halo(True).wait_recv()

            mix(kk - 1, 0, 64)

        return carry

    lax.fori_loop(0, kk - 1, third, 0)

    @pl.when((h > 0) & (h != middle))
    def _():
        halo(False).wait_recv()

    def ending(n, carry):
        base = pl.multiple_of(n * 32, 32)
        all_second(last_k, base, 32, kk - 1 + n).wait_recv()
        finish(last_k, base, 32)

        def rest(k, carry):
            mix(k, base, 32)
            return carry

        lax.fori_loop(jnp.where(is_high, 1, 0), kk - 1, rest, 0)
        return carry

    lax.fori_loop(0, 2, ending, 0)

    @pl.when(is_high)
    def _():
        halo(False).wait_recv()

    @pl.when(is_low)
    def _():
        halo(True).wait_recv()

    @pl.when(is_high | is_low)
    def _():
        mix(jnp.where(is_low, kk - 1, 0), 0, 64)

    def drain(i, carry):
        k = order(i)
        all_first(k).wait_send()

        @pl.when(i < kk - 1)
        def _():
            all_second(k, 0, 64, i).wait_send()

        return carry

    lax.fori_loop(0, kk, drain, 0)

    def drain_last(n, carry):
        base = pl.multiple_of(n * 32, 32)
        all_second(last_k, base, 32, kk - 1 + n).wait_send()
        return carry

    lax.fori_loop(0, 2, drain_last, 0)

    @pl.when(h > 0)
    def _():
        halo(True).wait_send()

    @pl.when(h < n_hel - 1)
    def _():
        halo(False).wait_send()

    @pl.when(carries_down)
    def _():
        hand_on(True).wait_send()

    @pl.when(carries_up)
    def _():
        hand_on(False).wait_send()


def solution(mesh):
    n_hel, n_rad = mesh.shape["hel"], mesh.shape["rad"]

    def per_device(packet, first, second, potential, coupling, weight):
        hbm = pl.BlockSpec(memory_space=pltpu.HBM)
        dma = pltpu.SemaphoreType.DMA
        return pl.pallas_call(
            functools.partial(kernel, n_hel, n_rad),
            out_shape=pltpu.VMEM(packet.shape, BF16),
            in_specs=[hbm] * 6,
            out_specs=pl.BlockSpec(memory_space=pltpu.VMEM),
            scratch_shapes=[
                pltpu.VMEM((4, 2, 64, 4, 512), BF16),
                pltpu.VMEM((256, 1024), BF16),
                pltpu.VMEM((2, 512, 512), BF16),
                pltpu.VMEM((1024, 1024), BF16),
                pltpu.VMEM((2, 1024, 1024), BF16),
                pltpu.VMEM((2, 1024, 1024), BF16),
                pltpu.VMEM((64, 4, 512), F32),
                pltpu.VMEM((4, 4, 64, 128), F32),
                pltpu.VMEM((4, 4, 64, 128), F32),
                pltpu.VMEM((64, 512), F32),
                pltpu.SMEM((4, 64), F32),
                pltpu.VMEM((8, 256, 128), F32),
                pltpu.VMEM((4, 16, 64, 256), BF16),
                pltpu.VMEM((4, 16, 64, 256), BF16),
                pltpu.VMEM((4, 16, 64, 256), BF16),
                pltpu.VMEM((4, 16, 64, 256), BF16),
                pltpu.VMEM((256, 1024), BF16),
                pltpu.VMEM((6, 256, 1024), BF16),
                pltpu.VMEM((64, 1024), BF16),
                dma((5,)),
                dma((4, 2)),
                dma((4,)),
                dma((4,)),
                dma((5,)),
                dma((5,)),
                dma((2,)),
                dma((2,)),
                dma,
                dma,
            ],
            compiler_params=pltpu.CompilerParams(
                collective_id=0,
                has_side_effects=True,
                vmem_limit_bytes=48 * 2**20,
            ),
        )(
            *(
                pltpu.with_memory_space_constraint(a, pltpu.HBM)
                for a in (coupling.T, packet, first, second, potential, weight)
            )
        )

    return jax.shard_map(
        per_device,
        mesh=mesh,
        in_specs=(
            P("rad", None, "hel", None, None),
            P(),
            P(),
            P("rad", None, None),
            P(),
            P("rad", None),
        ),
        out_specs=P("rad", None, "hel", None, None),
        check_vma=False,
    )
```

time: 119 us -> 107 us (0.90)
  Pallas kernels: 112 us -> 105 us
  local copies, waits for them, and re-layouts: 6.02 us -> 1.32 us
    pallas_call x1, Pallas kernels: 112 us -> 105 us  [per_device(): pl.pallas_call(functools.partial(kernel, n_hel, n_rad), out_shape=pltpu.V...]
    unnamed x2 -> x1, local copies, waits for them, and re-layouts: 6.02 us -> 1.32 us
where the time goes in v2:
time: 107 us
  Pallas kernels  105 us (98%)
  local copies, waits for them, and re-layouts  1.32 us (1%)
    pallas_call x1, Pallas kernels, per_device(): pl.pallas_call(functools.partial(kernel, n_hel, n_rad), out_shape=pltpu.V...  105 us

profile of v2, /device:TPU:32, one launch (start us, length us, event | category | flops | bytes accessed | tf_op | source)
XLA Modules:
  0.0 106.8 jit_solution(13260265887547675652)
XLA Ops:
  0.0 105.4 %shard_map.64 = bf16[64,2,4,4,512]{4,3,2,1,0:T(4,128)(2,1)S(1)} custom-call(f32[4,64]{1,0:T(4,128)} %bitcast.1, bf16[64,2,4,4,512]{4,3,2,1,0:T(4,128)(2,1)} %pk.1, bf16[2,1024,1024]{2,1,0:T(8,128)(2,1)} %p1.1, bf16[2,512,512]{2,1,0:T(8,128)(2,1)} %p2.1, f32[64,4,512]{2,1,0:T(4,128)} %pot.1, f32[64,512]{1,0:T(8,128)} %rw.1), custom_call_target="tpu_custom_call" | custom-call | tf_op jit(solution)/shard_map/pallas_call | solution.py:506
  105.4 1.3 %copy.8 = bf16[64,2,4,4,512]{4,3,2,1,0:T(4,128)(2,1)} copy(bf16[64,2,4,4,512]{4,3,2,1,0:T(4,128)(2,1)S(1)} %shard_map.64) | data formatting | bytes 4194304

commit v3 on v2

v3 whole, which is shorter than its diff:
```python
import functools

import jax
import jax.numpy as jnp
from jax import lax
from jax.experimental import pallas as pl
from jax.experimental.pallas import tpu as pltpu
from jax.sharding import PartitionSpec as P

MESH = pl.DeviceIdType.MESH
BF16 = jnp.bfloat16
F32 = jnp.float32
HALF = 32


def place_of(j, s):
    return j * 4 + (s - j) % 4


def phase(moved, cosv, sinv, ph, base, count):
    here = slice(base, base + count)
    for j in range(4):
        rows = slice(j * count, (j + 1) * count)
        for s in range(4):
            p = place_of(j, s)
            re, im = moved[p, here, :128].astype(F32), moved[p, here, 128:].astype(F32)
            c, sn = cosv[j, s, here], sinv[j, s, here]
            ph[rows, s * 128 : (s + 1) * 128] = (re * c + im * sn).astype(BF16)
            ph[rows, 512 + s * 128 : 512 + (s + 1) * 128] = (im * c - re * sn).astype(
                BF16
            )


def propagate(ph, pbig, wide, count):
    for s in range(4):
        y = jnp.dot(
            ph[: 4 * count],
            pbig[:, s * 256 : (s + 1) * 256],
            preferred_element_type=F32,
        )
        for c in range(2):
            for j in range(4):
                wide.at[c][pl.ds(s * 4 + j, count, stride=16), :] = y[
                    j * count : (j + 1) * count, c * 128 : (c + 1) * 128
                ]


def combine(q, base, wide, part, wu, wd, res):
    new, rows = chunk(q), chunk(q, base)
    re = wide[0, new].astype(BF16).astype(F32)
    im = wide[1, new].astype(BF16).astype(F32)
    up, down = wu[rows], wd[rows]
    values = (
        (part[0, 0, rows] + up * im, part[0, 1, rows] - up * re),
        (part[1, 0, rows] + re, part[1, 1, rows] + im),
        (part[2, 0, rows] + down * im, part[2, 1, rows] - down * re),
    )
    for n in range(3):
        for c in range(2):
            res[n, c, pl.ds(pl.multiple_of(q * 16, 16), 16)] = (
                values[n][c].astype(BF16).reshape(16, 16, 128)
            )


def tiles(x):
    return x.astype(F32).reshape(32, 8, 128)


def flat(x):
    return x.reshape(256, 128)


def chunk(q, base=0):
    return pl.ds(pl.multiple_of(base + q * 256, 256), 256)


def last_rows(
    n_hel,
    early,
    done,
    pbig,
    moved,
    cosv,
    sinv,
    part,
    wu,
    wd,
    out,
    ph,
    wide,
    res,
    sems,
):
    z_lo = lax.axis_index("hel") // (n_hel // 2)
    low = 1 - z_lo

    def put_early(c):
        return pltpu.make_async_copy(early.at[c], out.at[:, c, 3 * z_lo], sems.at[12 + c])

    def put_done(n, c):
        return pltpu.make_async_copy(
            done.at[n, c], out.at[pl.ds(0, HALF), c, low + n], sems.at[14 + 2 * n + c]
        )

    def put_rows(q, n, c):
        return pltpu.make_async_copy(
            res.at[n, c, pl.ds(pl.multiple_of(q * 16, 16), 16)],
            out.at[pl.ds(pl.multiple_of(HALF + q * 16, 16), 16), c, low + n],
            sems.at[q * 6 + 2 * n + c],
        )

    for c in range(2):
        put_early(c).start()
        for n in range(3):
            put_done(n, c).start()
    phase(moved, cosv, sinv, ph, HALF, HALF)
    propagate(ph, pbig, wide, HALF)

    def block(q, carry):
        combine(q, HALF * 16, wide, part, wu, wd, res)
        for n in range(3):
            for c in range(2):
                put_rows(q, n, c).start()
        return carry

    lax.fori_loop(0, 2, block, 0)

    def drain(q, carry):
        for n in range(3):
            for c in range(2):
                put_rows(q, n, c).wait()
        return carry

    lax.fori_loop(0, 2, drain, 0)
    for c in range(2):
        put_early(c).wait()
        for n in range(3):
            put_done(n, c).wait()


def kernel(
    n_hel,
    n_rad,
    coup_hbm,
    pk,
    p1,
    p2,
    pot,
    rw,
    early,
    done,
    pbig,
    mvl,
    cosv,
    sinv,
    part,
    wu,
    wd,
    pkv,
    p2v,
    p1v,
    p1t,
    potv,
    wv,
    wr,
    coup,
    fscr,
    wide,
    hs,
    cols,
    ps,
    mv,
    ph,
    kin,
    relay,
    load_sem,
    pk_sem,
    send1,
    recv1,
    send2,
    recv2,
    hsend,
    hrecv,
    rsend,
    rrecv,
):
    kk = pkv.shape[0]
    h = lax.axis_index("hel")
    r = lax.axis_index("rad")
    middle = n_hel // 2
    partner = lax.rem(h + middle, n_hel)
    zh, y = r // 4, lax.rem(r, 4)
    z_lo = h // middle

    def order(i):
        return jnp.where(z_lo == 0, lax.rem(3 + i, 4), lax.rem(3 * i, 4))

    def peer(i):
        b = i // 4
        dy = jnp.where(b == 0, 2, jnp.where(b == 3, 0, 2 * b - 1))
        return lax.rem(zh + lax.rem(i, 4) + 1 + z_lo, 4) * 4 + lax.rem(y + dy, 4)

    is_low, is_high = h == middle - 1, h == middle
    carries_down = (h > middle + 1) & (lax.rem(h, 2) == 1)
    carries_up = (h < middle - 2) & (lax.rem(h, 2) == 1)

    barrier = pltpu.get_barrier_semaphore()

    def greet_one(target, rad):
        pl.semaphore_signal(
            barrier, inc=1, device_id=(target, rad), device_id_type=MESH
        )

    def greet(i, carry):
        greet_one(partner, peer(i))
        return carry

    lax.fori_loop(0, n_rad, greet, 0)

    @pl.when(h > 0)
    def _():
        greet_one(h - 1, r)

    @pl.when(h < n_hel - 1)
    def _():
        greet_one(h + 1, r)

    @pl.when(carries_down)
    def _():
        greet_one(middle, r)

    @pl.when(carries_up)
    def _():
        greet_one(middle - 1, r)

    @pl.when(is_low)
    def _():
        for q in range(1, 4):
            greet_one(middle + 2 * q + 1, r)

    @pl.when(is_high)
    def _():
        for q in range(3):
            greet_one(2 * q + 1, r)

    greeted = n_rad + jnp.where(h > 0, 1, 0) + jnp.where(h < n_hel - 1, 1, 0)
    greeted += jnp.where(is_low | is_high, 3, 0)
    greeted += jnp.where(carries_down | carries_up, 1, 0)

    def load_packet(i):
        k = order(i)
        return [
            pltpu.make_async_copy(pk.at[:, c, k], pkv.at[k, c], pk_sem.at[i, c])
            for c in range(2)
        ]

    load_p2 = pltpu.make_async_copy(p2, p2v, load_sem.at[0])
    load_p1 = pltpu.make_async_copy(p1, p1v, load_sem.at[1])
    load_pot = pltpu.make_async_copy(pot, potv, load_sem.at[2])
    load_w = pltpu.make_async_copy(rw, wv, load_sem.at[3])
    load_coup = pltpu.make_async_copy(coup_hbm, coup, load_sem.at[4])
    load_p2.start()
    for i in range(kk):
        for copy in load_packet(i):
            copy.start()
    load_p1.start()
    load_pot.start()
    load_w.start()
    load_coup.start()

    load_p2.wait()

    def first(i, carry):
        k = order(i)
        for copy in load_packet(i):
            copy.wait()
        x = [pkv[k, c].reshape(256, 512) for c in range(2)]
        for t in range(2):
            lanes = slice(t * 256, (t + 1) * 256)

            def product(c, d):
                return jnp.dot(x[c], p2v[d, :, lanes], preferred_element_type=F32)

            real = product(0, 0) - product(1, 1)
            imag = product(0, 1) + product(1, 0)
            for s in range(2):
                fscr[4 * t + 2 * s] = real[:, s * 128 : (s + 1) * 128]
                fscr[4 * t + 2 * s + 1] = imag[:, s * 128 : (s + 1) * 128]
            for j in range(4):
                for s in (2 * t, 2 * t + 1):
                    for c in range(2):
                        rows = fscr.at[2 * s + c][pl.ds(j, 64, stride=4), :]
                        hs[i, place_of(j, s), :, c * 128 : (c + 1) * 128] = rows.astype(
                            BF16
                        )

        @pl.when(i == 0)
        def _():
            pl.semaphore_wait(barrier, greeted)

        def send(n, carry):
            p = peer(n)
            pltpu.make_async_remote_copy(
                src_ref=hs.at[i, p],
                dst_ref=cols.at[i, r],
                send_sem=send1.at[i],
                recv_sem=recv1.at[i],
                device_id=(partner, p),
                device_id_type=MESH,
            ).start()
            return carry

        lax.fori_loop(0, n_rad, send, 0)
        return carry

    lax.fori_loop(0, kk, first, 0)

    for s in range(4):
        lanes = slice(s * 128, (s + 1) * 128)
        real, imag = p2v[0, :, lanes], p2v[1, :, lanes]
        pbig[:512, s * 256 : s * 256 + 128] = real
        pbig[:512, s * 256 + 128 : (s + 1) * 256] = imag
        pbig[512:, s * 256 : s * 256 + 128] = -imag
        pbig[512:, s * 256 + 128 : (s + 1) * 256] = real

    load_p1.wait()

    def flip(n, carry):
        rows = pl.ds(pl.multiple_of(n * 128, 128), 128)
        for c in range(2):
            p1t[c, rows, :] = p1v[c, :, rows].T
        return carry

    lax.fori_loop(0, 8, flip, 0)
    load_pot.wait()
    for s in range(4):
        fscr[s] = potv[:, :, s * 128 : (s + 1) * 128].reshape(256, 128)

    def phases(s, carry):
        for j in range(4):
            angle = fscr.at[s][pl.ds(j, 64, stride=4), :]
            cosv[j, s] = jnp.cos(angle)
            sinv[j, s] = jnp.sin(angle)
        return carry

    lax.fori_loop(0, 4, phases, 0)
    load_w.wait()
    load_coup.wait()
    for s in range(4):
        for j in range(4):
            wr[pl.ds(s * 4 + j, 64, stride=16), :] = wv[:, s * 128 : (s + 1) * 128]

    def whole(src, dst, send_sem, recv_sem):
        return pltpu.make_async_remote_copy(
            src_ref=src,
            dst_ref=dst,
            send_sem=send_sem,
            recv_sem=recv_sem,
            device_id=(partner, r),
            device_id_type=MESH,
        )

    def all_first(k):
        return whole(hs.at[k], cols.at[k], send1.at[k], recv1.at[k])

    def all_second(i):
        return whole(ps.at[i], mv.at[i], send2.at[i], recv2.at[i])

    def all_last(n):
        part = pl.ds(n * HALF, HALF)
        return whole(
            ps.at[3, :, part], mvl.at[:, part], send2.at[3 + n], recv2.at[3 + n]
        )

    def left(k):
        all_first(k).wait_recv()

        def block(n, carry):
            rows = pl.ds(pl.multiple_of(n * 256, 256), 256)
            u = cols[k].reshape(1024, 256)
            a = jnp.dot(p1t[0, rows, :], u, preferred_element_type=F32)
            b = jnp.dot(p1t[1, rows, :], u, preferred_element_type=F32)
            real = a[:, :128] - b[:, 128:]
            imag = a[:, 128:] + b[:, :128]
            four = pl.ds(n * 4, 4)
            ps[k, four, :, :128] = real.astype(BF16).reshape(4, 64, 128)
            ps[k, four, :, 128:] = imag.astype(BF16).reshape(4, 64, 128)
            return carry

        lax.fori_loop(0, 4, block, 0)

    def send_back(i, there):
        def send(n, carry):
            p = peer(n)
            pltpu.make_async_remote_copy(
                src_ref=ps.at[i, p],
                dst_ref=there.at[r],
                send_sem=send2.at[i],
                recv_sem=recv2.at[i],
                device_id=(partner, p),
                device_id_type=MESH,
            ).start()
            return carry

        lax.fori_loop(0, n_rad, send, 0)

    def second(i, carry):
        left(i)
        send_back(i, mv.at[i])
        return carry

    lax.fori_loop(0, kk - 1, second, 0)

    @pl.when(h == 0)
    def _():
        kin[0] = jnp.zeros_like(kin[0])

    @pl.when(h == n_hel - 1)
    def _():
        kin[kk + 1] = jnp.zeros_like(kin[kk + 1])

    def ends(low):
        return (1, kk + 1, 0) if low else (kk, 0, 1)

    def halo(low):
        own, there, n = ends(low)
        return pltpu.make_async_remote_copy(
            src_ref=kin.at[own],
            dst_ref=kin.at[there],
            send_sem=hsend.at[n],
            recv_sem=hrecv.at[n],
            device_id=(h - 1 if low else h + 1, r),
            device_id_type=MESH,
        )

    def quarter(low, q, target, by_helper):
        own, there, n = ends(low)
        rows = pl.ds(q * 512, 512)
        return pltpu.make_async_remote_copy(
            src_ref=kin.at[own, rows],
            dst_ref=relay if by_helper else kin.at[there, rows],
            send_sem=hsend.at[n],
            recv_sem=rrecv if by_helper else hrecv.at[n],
            device_id=(target, r),
            device_id_type=MESH,
        )

    def hand_on(low):
        own, there, n = ends(low)
        q = (h - middle - 1) // 2 if low else (h - 1) // 2
        rows = pl.ds(pl.multiple_of(q * 512, 512), 512)
        return pltpu.make_async_remote_copy(
            src_ref=relay,
            dst_ref=kin.at[there, rows],
            send_sem=rsend,
            recv_sem=hrecv.at[n],
            device_id=(middle - 1 if low else middle, r),
            device_id_type=MESH,
        )

    def arrived_at_helper(low):
        return quarter(low, 0, partner, True)

    def factors(k):
        g = h * kk + k
        row = lax.broadcasted_iota(jnp.int32, (8, 128), 0) % 4
        up, down = jnp.zeros((8, 128), F32), jnp.zeros((8, 128), F32)
        for j in range(4):
            to_up = jnp.where(g < n_hel * kk - 1, coup[j, g], 0.0)
            to_down = jnp.where(g > 0, coup[j, jnp.maximum(g - 1, 0)], 0.0)
            up = jnp.where(row == j, to_up, up)
            down = jnp.where(row == j, to_down, down)
        return up, down

    def at(slot, c, q):
        return tiles(kin[slot, chunk(q, c * 1024)])

    def finish(i):
        phase(mv.at[i], cosv, sinv, ph, 0, 64)
        propagate(ph, pbig, wide, 64)

        def store(q, carry):
            for c in range(2):
                kin[order(i) + 1, chunk(q, c * 1024)] = wide[c, chunk(q)].astype(BF16)
            return carry

        lax.fori_loop(0, 4, store, 0)

    def mix_early():
        k = 3 * z_lo
        up, down = factors(k)

        def block(q, carry):
            w = tiles(wr[chunk(q)])
            by = [w * (up * at(k + 2, c, q) + down * at(k, c, q)) for c in range(2)]
            rows = pl.ds(pl.multiple_of(q * 16, 16), 16)
            for c, x in enumerate((at(k + 1, 0, q) + by[1], at(k + 1, 1, q) - by[0])):
                early[c, rows] = flat(x).astype(BF16).reshape(16, 16, 128)
            return carry

        lax.fori_loop(0, 4, block, 0)

    low = 1 - z_lo

    def put_part(n, q, real, imag):
        part[n, 0, chunk(q)] = flat(real)
        part[n, 1, chunk(q)] = flat(imag)

    def part_first():
        up, down = factors(low)

        def block(q, carry):
            w = tiles(wr[chunk(q)])
            by = [w * (down * at(low, c, q)) for c in range(2)]
            put_part(0, q, at(low + 1, 0, q) + by[1], at(low + 1, 1, q) - by[0])
            wu[chunk(q)] = flat(w * up)
            return carry

        lax.fori_loop(0, 4, block, 0)

    def part_middle():
        up, down = factors(low + 1)

        def block(q, carry):
            w = tiles(wr[chunk(q)])
            by = [
                w * (up * at(low + 3, c, q) + down * at(low + 1, c, q))
                for c in range(2)
            ]
            put_part(1, q, by[1], -by[0])
            return carry

        lax.fori_loop(0, 4, block, 0)

    def part_last():
        up, down = factors(low + 2)

        def block(q, carry):
            w = tiles(wr[chunk(q)])
            by = [w * (up * at(low + 4, c, q)) for c in range(2)]
            put_part(2, q, at(low + 3, 0, q) + by[1], at(low + 3, 1, q) - by[0])
            wd[chunk(q)] = flat(w * down)
            return carry

        lax.fori_loop(0, 4, block, 0)

    def third(i):
        all_second(i).wait_recv()
        finish(i)

    def send_edge(low):
        @pl.when((h > 0) & (h != middle) if low else (h < n_hel - 1) & (h != middle - 1))
        def _():
            halo(low).start()

        @pl.when(is_high if low else is_low)
        def _():
            for q in range(4):
                if q == (0 if low else 3):
                    quarter(low, q, middle - 1 if low else middle, False).start()
                else:
                    helper = middle + 2 * q + 1 if low else 2 * q + 1
                    quarter(low, q, helper, True).start()

    third(0)

    @pl.when(z_lo == 1)
    def _():
        send_edge(True)

    @pl.when(z_lo == 0)
    def _():
        send_edge(False)

    @pl.when(carries_down)
    def _():
        arrived_at_helper(True).wait_recv()
        hand_on(True).start()

    @pl.when(carries_up)
    def _():
        arrived_at_helper(False).wait_recv()
        hand_on(False).start()

    left(kk - 1)
    for batch in range(2):
        half = pl.ds(batch * HALF, HALF)

        def send(n, carry):
            p = peer(n)
            pltpu.make_async_remote_copy(
                src_ref=ps.at[kk - 1, p, half],
                dst_ref=mvl.at[r, half],
                send_sem=send2.at[kk - 1 + batch],
                recv_sem=recv2.at[kk - 1 + batch],
                device_id=(partner, p),
                device_id_type=MESH,
            ).start()
            return carry

        lax.fori_loop(0, n_rad, send, 0)

    third(1)

    @pl.when(z_lo == 1)
    def _():
        send_edge(False)

    @pl.when(z_lo == 0)
    def _():
        send_edge(True)

    third(2)

    @pl.when((z_lo == 1) & (h < n_hel - 1))
    def _():
        halo(True).wait_recv()

    @pl.when((z_lo == 0) & (h > 0))
    def _():
        halo(False).wait_recv()

    mix_early()
    part_middle()

    @pl.when(z_lo == 1)
    def _():
        part_last()
        halo(False).wait_recv()
        part_first()

    @pl.when(z_lo == 0)
    def _():
        part_first()
        halo(True).wait_recv()
        part_last()

    all_last(0).wait_recv()
    phase(mvl, cosv, sinv, ph, 0, HALF)
    propagate(ph, pbig, wide, HALF)

    def first_rows(q, carry):
        combine(q, 0, wide, part, wu, wd, done)
        return carry

    lax.fori_loop(0, 2, first_rows, 0)
    all_last(1).wait_recv()

    def drain(i, carry):
        all_first(i).wait_send()
        return carry

    lax.fori_loop(0, kk, drain, 0)

    for i in range(kk - 1):
        all_second(i).wait_send()
    for batch in range(2):
        all_last(batch).wait_send()

    @pl.when(h > 0)
    def _():
        halo(True).wait_send()

    @pl.when(h < n_hel - 1)
    def _():
        halo(False).wait_send()

    @pl.when(carries_down)
    def _():
        hand_on(True).wait_send()

    @pl.when(carries_up)
    def _():
        hand_on(False).wait_send()


def solution(mesh):
    n_hel, n_rad = mesh.shape["hel"], mesh.shape["rad"]

    def per_device(packet, first, second, potential, coupling, weight):
        hbm = pl.BlockSpec(memory_space=pltpu.HBM)
        vmem = pl.BlockSpec(memory_space=pltpu.VMEM)
        dma = pltpu.SemaphoreType.DMA
        state = pl.pallas_call(
            functools.partial(kernel, n_hel, n_rad),
            out_shape=(
                pltpu.VMEM((2, 64, 16, 128), BF16),
                pltpu.VMEM((3, 2, HALF, 16, 128), BF16),
                pltpu.VMEM((1024, 1024), BF16),
                pltpu.VMEM((16, 64, 256), BF16),
                pltpu.VMEM((4, 4, 64, 128), F32),
                pltpu.VMEM((4, 4, 64, 128), F32),
                pltpu.VMEM((3, 2, 1024, 128), F32),
                pltpu.VMEM((1024, 128), F32),
                pltpu.VMEM((1024, 128), F32),
            ),
            in_specs=[hbm] * 6,
            out_specs=[vmem] * 9,
            scratch_shapes=[
                pltpu.VMEM((4, 2, 64, 4, 512), BF16),
                pltpu.VMEM((2, 512, 512), BF16),
                pltpu.VMEM((2, 1024, 1024), BF16),
                pltpu.VMEM((2, 1024, 1024), BF16),
                pltpu.VMEM((64, 4, 512), F32),
                pltpu.VMEM((64, 512), F32),
                pltpu.VMEM((1024, 128), F32),
                pltpu.SMEM((4, 64), F32),
                pltpu.VMEM((8, 256, 128), F32),
                pltpu.VMEM((2, 1024, 128), F32),
                pltpu.VMEM((4, 16, 64, 256), BF16),
                pltpu.VMEM((4, 16, 64, 256), BF16),
                pltpu.VMEM((4, 16, 64, 256), BF16),
                pltpu.VMEM((3, 16, 64, 256), BF16),
                pltpu.VMEM((256, 1024), BF16),
                pltpu.VMEM((6, 2048, 128), BF16),
                pltpu.VMEM((512, 128), BF16),
                dma((5,)),
                dma((4, 2)),
                dma((4,)),
                dma((4,)),
                dma((5,)),
                dma((5,)),
                dma((2,)),
                dma((2,)),
                dma,
                dma,
            ],
            compiler_params=pltpu.CompilerParams(
                collective_id=0,
                has_side_effects=True,
                vmem_limit_bytes=48 * 2**20,
            ),
        )(
            *(
                pltpu.with_memory_space_constraint(a, pltpu.HBM)
                for a in (coupling.T, packet, first, second, potential, weight)
            )
        )
        rows = pl.pallas_call(
            functools.partial(last_rows, n_hel),
            out_shape=pltpu.HBM((64, 2, 4, 16, 128), BF16),
            in_specs=[vmem] * 9,
            out_specs=hbm,
            scratch_shapes=[
                pltpu.VMEM((4 * HALF, 1024), BF16),
                pltpu.VMEM((2, HALF * 16, 128), F32),
                pltpu.VMEM((3, 2, HALF, 16, 128), BF16),
                dma((20,)),
            ],
            compiler_params=pltpu.CompilerParams(vmem_limit_bytes=16 * 2**20),
        )(*(pltpu.with_memory_space_constraint(a, pltpu.VMEM) for a in state))
        rows = rows.reshape(64, 2, 4, 4, 4, 128)
        return rows.transpose(0, 1, 2, 4, 3, 5).reshape(packet.shape)

    return jax.shard_map(
        per_device,
        mesh=mesh,
        in_specs=(
            P("rad", None, "hel", None, None),
            P(),
            P(),
            P("rad", None, None),
            P(),
            P("rad", None),
        ),
        out_specs=P("rad", None, "hel", None, None),
        check_vma=False,
    )
```

time: 107 us -> 105 us (0.981)
  the two profiles are of different devices: /device:TPU:32 before, /device:TPU:5 now
where the time goes in v3:
time: 105 us
  Pallas kernels  105 us (100%)
    pallas_call x1, Pallas kernels, per_device(): pl.pallas_call(functools.partial(kernel, n_hel, n_rad), out_shape=(pltpu....  103 us

profile of v3, /device:TPU:5, one launch (start us, length us, event | category | flops | bytes accessed | tf_op | source)
XLA Modules:
  0.0 105.0 jit_solution(5852155876006248383)
XLA Ops:
  0.0 103.1 %shard_map.64 = (bf16[2,64,16,128]{3,2,1,0:T(8,128)(2,1)S(1)}, bf16[3,2,32,16,128]{4,3,2,1,0:T(8,128)(2,1)S(1)}, bf16[1024,1024]{1,0:T(8,128)(2,1)S(1)}, bf16[16...) custom-call(f32[4,64]{1,0:T(4,128)} %bitcast.6, ...), custom_call_target="tpu_custom_call" | custom-call | tf_op jit(solution)/shard_map/pallas_call | solution.py:684
  103.2 1.8 %shard_map.65 = bf16[64,2,4,16,128]{4,3,2,1,0:T(8,128)(2,1)} custom-call(bf16[2,64,16,128]{3,2,1,0:T(8,128)(2,1)S(1)} %get-tuple-element.14.early, bf16[3,2,32,16,128]{4,3,2,1,0:T(8,128)(2,1)S(1)} %get-tuple-element.15.done, bf16[1024,1024]{1,0:T(8,128)(2,1)S(1)} %get-tuple-element.16.pbig, bf16[16,64,256]{2,1,0:T(8,128)(2,1)S(1)} %get-tuple-element.17.moved, ...), custom_call_target="tpu_custom_call" | custom-call | tf_op jit(solution)/shard_map/pallas_call | solution.py:739

commit v4 on v3

--- a/solution.py
+++ b/solution.py
@@ -10,7 +10,8 @@
 MESH = pl.DeviceIdType.MESH
 BF16 = jnp.bfloat16
 F32 = jnp.float32
-HALF = 32
+BATCHES = ((0, 32), (32, 32))
+MOST, REST = BATCHES[-1]
 
 
 def place_of(j, s):
@@ -45,8 +46,8 @@
                 ]
 
 
-def combine(q, base, wide, part, wu, wd, res):
-    new, rows = chunk(q), chunk(q, base)
+def combine(q, base, first, low, wide, part, wu, wd, res):
+    new, rows = chunk(q), chunk(q, base * 16)
     re = wide[0, new].astype(BF16).astype(F32)
     im = wide[1, new].astype(BF16).astype(F32)
     up, down = wu[rows], wd[rows]
@@ -57,7 +58,7 @@
     )
     for n in range(3):
         for c in range(2):
-            res[n, c, pl.ds(pl.multiple_of(q * 16, 16), 16)] = (
+            res[pl.ds(first + q * 16, 16), c, low + n] = (
                 values[n][c].astype(BF16).reshape(16, 16, 128)
             )
 
@@ -76,7 +77,6 @@
 
 def last_rows(
     n_hel,
-    early,
     done,
     pbig,
     moved,
@@ -94,48 +94,25 @@
     z_lo = lax.axis_index("hel") // (n_hel // 2)
     low = 1 - z_lo
 
-    def put_early(c):
-        return pltpu.make_async_copy(early.at[c], out.at[:, c, 3 * z_lo], sems.at[12 + c])
-
-    def put_done(n, c):
-        return pltpu.make_async_copy(
-            done.at[n, c], out.at[pl.ds(0, HALF), c, low + n], sems.at[14 + 2 * n + c]
-        )
-
-    def put_rows(q, n, c):
-        return pltpu.make_async_copy(
-            res.at[n, c, pl.ds(pl.multiple_of(q * 16, 16), 16)],
-            out.at[pl.ds(pl.multiple_of(HALF + q * 16, 16), 16), c, low + n],
-            sems.at[q * 6 + 2 * n + c],
-        )
-
+    copies = [
+        pltpu.make_async_copy(
+            done.at[pl.ds(n * 16, 16)], out.at[pl.ds(n * 16, 16)], sems.at[n]
+        )
+        for n in range(MOST // 16)
+    ]
+    for copy in copies:
+        copy.start()
+    phase(moved, cosv, sinv, ph, MOST, REST)
     for c in range(2):
-        put_early(c).start()
-        for n in range(3):
-            put_done(n, c).start()
-    phase(moved, cosv, sinv, ph, HALF, HALF)
-    propagate(ph, pbig, wide, HALF)
-
-    def block(q, carry):
-        combine(q, HALF * 16, wide, part, wu, wd, res)
-        for n in range(3):
-            for c in range(2):
-                put_rows(q, n, c).start()
-        return carry
-
-    lax.fori_loop(0, 2, block, 0)
-
-    def drain(q, carry):
-        for n in range(3):
-            for c in range(2):
-                put_rows(q, n, c).wait()
-        return carry
-
-    lax.fori_loop(0, 2, drain, 0)
-    for c in range(2):
-        put_early(c).wait()
-        for n in range(3):
-            put_done(n, c).wait()
+        res[:, c, 3 * z_lo] = done[MOST:, c, 3 * z_lo]
+    propagate(ph, pbig, wide, REST)
+    for q in range(REST // 16):
+        combine(q, MOST, 0, low, wide, part, wu, wd, res)
+    last = pltpu.make_async_copy(res, out.at[pl.ds(MOST, REST)], sems.at[3])
+    last.start()
+    for copy in copies:
+        copy.wait()
+    last.wait()
 
 
 def kernel(
@@ -147,7 +124,6 @@
     p2,
     pot,
     rw,
-    early,
     done,
     pbig,
     mvl,
@@ -367,7 +343,7 @@
         return whole(ps.at[i], mv.at[i], send2.at[i], recv2.at[i])
 
     def all_last(n):
-        part = pl.ds(n * HALF, HALF)
+        part = pl.ds(*BATCHES[n])
         return whole(
             ps.at[3, :, part], mvl.at[:, part], send2.at[3 + n], recv2.at[3 + n]
         )
@@ -495,7 +471,7 @@
             by = [w * (up * at(k + 2, c, q) + down * at(k, c, q)) for c in range(2)]
             rows = pl.ds(pl.multiple_of(q * 16, 16), 16)
             for c, x in enumerate((at(k + 1, 0, q) + by[1], at(k + 1, 1, q) - by[0])):
-                early[c, rows] = flat(x).astype(BF16).reshape(16, 16, 128)
+                done[rows, c, k] = flat(x).astype(BF16).reshape(16, 16, 128)
             return carry
 
         lax.fori_loop(0, 4, block, 0)
@@ -583,14 +559,14 @@
         hand_on(False).start()
 
     left(kk - 1)
-    for batch in range(2):
-        half = pl.ds(batch * HALF, HALF)
+    for batch, points in enumerate(BATCHES):
+        here = pl.ds(*points)
 
         def send(n, carry):
             p = peer(n)
             pltpu.make_async_remote_copy(
-                src_ref=ps.at[kk - 1, p, half],
-                dst_ref=mvl.at[r, half],
+                src_ref=ps.at[kk - 1, p, here],
+                dst_ref=mvl.at[r, here],
                 send_sem=send2.at[kk - 1 + batch],
                 recv_sem=recv2.at[kk - 1 + batch],
                 device_id=(partner, p),
@@ -635,16 +611,13 @@
         halo(True).wait_recv()
         part_last()
 
-    all_last(0).wait_recv()
-    phase(mvl, cosv, sinv, ph, 0, HALF)
-    propagate(ph, pbig, wide, HALF)
-
-    def first_rows(q, carry):
-        combine(q, 0, wide, part, wu, wd, done)
-        return carry
-
-    lax.fori_loop(0, 2, first_rows, 0)
-    all_last(1).wait_recv()
+    for batch, (base, count) in enumerate(BATCHES[:-1]):
+        all_last(batch).wait_recv()
+        phase(mvl, cosv, sinv, ph, base, count)
+        propagate(ph, pbig, wide, count)
+        for q in range(count // 16):
+            combine(q, base, base, low, wide, part, wu, wd, done)
+    all_last(len(BATCHES) - 1).wait_recv()
 
     def drain(i, carry):
         all_first(i).wait_send()
@@ -654,7 +627,7 @@
 
     for i in range(kk - 1):
         all_second(i).wait_send()
-    for batch in range(2):
+    for batch in range(len(BATCHES)):
         all_last(batch).wait_send()
 
     @pl.when(h > 0)
@@ -684,8 +657,7 @@
         state = pl.pallas_call(
             functools.partial(kernel, n_hel, n_rad),
             out_shape=(
-                pltpu.VMEM((2, 64, 16, 128), BF16),
-                pltpu.VMEM((3, 2, HALF, 16, 128), BF16),
+                pltpu.VMEM((64, 2, 4, 16, 128), BF16),
                 pltpu.VMEM((1024, 1024), BF16),
                 pltpu.VMEM((16, 64, 256), BF16),
                 pltpu.VMEM((4, 4, 64, 128), F32),
@@ -695,7 +667,7 @@
                 pltpu.VMEM((1024, 128), F32),
             ),
             in_specs=[hbm] * 6,
-            out_specs=[vmem] * 9,
+            out_specs=[vmem] * 8,
             scratch_shapes=[
                 pltpu.VMEM((4, 2, 64, 4, 512), BF16),
                 pltpu.VMEM((2, 512, 512), BF16),
@@ -739,13 +711,13 @@
         rows = pl.pallas_call(
             functools.partial(last_rows, n_hel),
             out_shape=pltpu.HBM((64, 2, 4, 16, 128), BF16),
-            in_specs=[vmem] * 9,
+            in_specs=[vmem] * 8,
             out_specs=hbm,
             scratch_shapes=[
-                pltpu.VMEM((4 * HALF, 1024), BF16),
-                pltpu.VMEM((2, HALF * 16, 128), F32),
-                pltpu.VMEM((3, 2, HALF, 16, 128), BF16),
-                dma((20,)),
+                pltpu.VMEM((4 * REST, 1024), BF16),
+                pltpu.VMEM((2, REST * 16, 128), F32),
+                pltpu.VMEM((REST, 2, 4, 16, 128), BF16),
+                dma((4,)),
             ],
             compiler_params=pltpu.CompilerParams(vmem_limit_bytes=16 * 2**20),
         )(*(pltpu.with_memory_space_constraint(a, pltpu.VMEM) for a in state))

time: 105 us -> 105 us (level)
  no operation moved by 1% of the time
where the time goes in v4:
time: 105 us
  Pallas kernels  105 us (100%)
    pallas_call x1, Pallas kernels, per_device(): pl.pallas_call(functools.partial(kernel, n_hel, n_rad), out_shape=(pltpu....  103 us

profile of v4, /device:TPU:5, one launch (start us, length us, event | category | flops | bytes accessed | tf_op | source)
XLA Modules:
  0.0 104.9 jit_solution(13186244306880329945)
XLA Ops:
  0.0 103.1 %shard_map.64 = (bf16[64,2,4,16,128]{4,3,2,1,0:T(8,128)(2,1)S(1)}, bf16[1024,1024]{1,0:T(8,128)(2,1)S(1)}, bf16[16,64,256]{2,1,0:T(8,128)(2,1)S(1)}, f32[4,4,64,...) custom-call(f32[4,64]{1,0:T(4,128)} %bitcast.6, ...), custom_call_target="tpu_custom_call" | custom-call | tf_op jit(solution)/shard_map/pallas_call | solution.py:657
  103.2 1.8 %shard_map.65 = bf16[64,2,4,16,128]{4,3,2,1,0:T(8,128)(2,1)} custom-call(bf16[64,2,4,16,128]{4,3,2,1,0:T(8,128)(2,1)S(1)} %get-tuple-element.13.done, bf16[1024,1024]{1,0:T(8,128)(2,1)S(1)} %get-tuple-element.14.pbig, bf16[16,64,256]{2,1,0:T(8,128)(2,1)S(1)} %get-tuple-element.15.moved, f32[4,4,64,128]{3,2,1,0:T(8,128)S(1)} %get-tuple-element.16.cosv, ...), custom_call_target="tpu_custom_call" | custom-call | tf_op jit(solution)/shard_map/pallas_call | solution.py:711

commit v5 on v4

--- a/solution.py
+++ b/solution.py
@@ -538,6 +538,31 @@
                     helper = middle + 2 * q + 1 if low else 2 * q + 1
                     quarter(low, q, helper, True).start()
 
+    on_the_way = is_low | is_high | carries_down | carries_up
+
+    def last_left():
+        left(kk - 1)
+        for batch, points in enumerate(BATCHES):
+            here = pl.ds(*points)
+
+            def send(n, carry):
+                p = peer(n)
+                pltpu.make_async_remote_copy(
+                    src_ref=ps.at[kk - 1, p, here],
+                    dst_ref=mvl.at[r, here],
+                    send_sem=send2.at[kk - 1 + batch],
+                    recv_sem=recv2.at[kk - 1 + batch],
+                    device_id=(partner, p),
+                    device_id_type=MESH,
+                ).start()
+                return carry
+
+            lax.fori_loop(0, n_rad, send, 0)
+
+    @pl.when(jnp.logical_not(on_the_way))
+    def _():
+        last_left()
+
     third(0)
 
     @pl.when(z_lo == 1)
@@ -558,23 +583,9 @@
         arrived_at_helper(False).wait_recv()
         hand_on(False).start()
 
-    left(kk - 1)
-    for batch, points in enumerate(BATCHES):
-        here = pl.ds(*points)
-
-        def send(n, carry):
-            p = peer(n)
-            pltpu.make_async_remote_copy(
-                src_ref=ps.at[kk - 1, p, here],
-                dst_ref=mvl.at[r, here],
-                send_sem=send2.at[kk - 1 + batch],
-                recv_sem=recv2.at[kk - 1 + batch],
-                device_id=(partner, p),
-                device_id_type=MESH,
-            ).start()
-            return carry
-
-        lax.fori_loop(0, n_rad, send, 0)
+    @pl.when(on_the_way)
+    def _():
+        last_left()
 
     third(1)
 

time: 105 us -> 105 us (level)
  no operation moved by 1% of the time
where the time goes in v5:
time: 105 us
  Pallas kernels  105 us (100%)
    pallas_call x1, Pallas kernels, per_device(): pl.pallas_call(functools.partial(kernel, n_hel, n_rad), out_shape=(pltpu....  103 us

profile of v5, /device:TPU:5, one launch (start us, length us, event | category | flops | bytes accessed | tf_op | source)
XLA Modules:
  0.0 104.9 jit_solution(1084944493908822920)
XLA Ops:
  0.0 103.1 %shard_map.64 = (bf16[64,2,4,16,128]{4,3,2,1,0:T(8,128)(2,1)S(1)}, bf16[1024,1024]{1,0:T(8,128)(2,1)S(1)}, bf16[16,64,256]{2,1,0:T(8,128)(2,1)S(1)}, f32[4,4,64,...) custom-call(f32[4,64]{1,0:T(4,128)} %bitcast.6, ...), custom_call_target="tpu_custom_call" | custom-call | tf_op jit(solution)/shard_map/pallas_call | solution.py:668
  103.2 1.8 %shard_map.65 = bf16[64,2,4,16,128]{4,3,2,1,0:T(8,128)(2,1)} custom-call(bf16[64,2,4,16,128]{4,3,2,1,0:T(8,128)(2,1)S(1)} %get-tuple-element.13.done, bf16[1024,1024]{1,0:T(8,128)(2,1)S(1)} %get-tuple-element.14.pbig, bf16[16,64,256]{2,1,0:T(8,128)(2,1)S(1)} %get-tuple-element.15.moved, f32[4,4,64,128]{3,2,1,0:T(8,128)S(1)} %get-tuple-element.16.cosv, ...), custom_call_target="tpu_custom_call" | custom-call | tf_op jit(solution)/shard_map/pallas_call | solution.py:722
